TPU v7x, 1024 devices: a whole 4x8x16 slice. The times are simulated.
1024 devices in a mesh: gx: 8 (over z_lo, core), gy: 16 (over z_hi, x), gz: 8 (over y).
Axes of the slice: x: 4, y: 8, z: 16 (z_hi: 4, z_lo: 4; z = z_hi * 4 + z_lo), core: 2. Of those that a mesh axis runs over, the one named last changes fastest.
Arguments:
- deflation: bfloat16 [64, 64, 32, 3, 128], P('gx', 'gy', 'gz'), may hold values from -0.33 to 0.33
- material: int32 [64, 64, 32], P('gx', 'gy', 'gz'), may hold values from 0 to 15
- moduli: float32 [16], replicated, may hold values from 1 to 100
- stencil: float32 [27, 3, 3], replicated, may hold values from -0.6 to 0.6
Outputs:
- coarse: float32 [8, 16, 128, 8, 27, 128], P('gx', 'gy', 'gz')
All inputs are finite; a program needn't handle non-finite values.
Results may differ from a plain program's by a relative error of at most 0.005.
Values may be sent and summed in bfloat16 or wider, within the bound.
A program may use at most 32 MiB of HBM per device.

v0:
```python
import functools

import jax
import jax.numpy as jnp
import numpy as np
from jax import lax
from jax.experimental import pallas as pl
from jax.experimental.pallas import tpu as pltpu
from jax.sharding import PartitionSpec as P

MESH = pl.DeviceIdType.MESH
HIGHEST = lax.Precision.HIGHEST
CX, CY, CZ, VECS = 8, 4, 4, 128
PLANE = CY * 3 * CZ
OFFSETS = [(i, j, k) for i in (-1, 0, 1) for j in (-1, 0, 1) for k in (-1, 0, 1)]
NEIGHBOURS = [o for o in OFFSETS if o != (0, 0, 0)]
GROUPS = (
    [(0, 0, 0)],
    [o for o in NEIGHBOURS if o[1] == 0],
    [o for o in NEIGHBOURS if o[1] != 0],
)
ORDER = [o for g in GROUPS for o in g]
STARTS = [sum(len(g) for g in GROUPS[:i]) for i in range(len(GROUPS))]


def number(o):
    return 9 * (o[0] + 1) + 3 * (o[1] + 1) + o[2] + 1


def side(v):
    return 1 if v > 0 else 0


def pair(v, w):
    return 2 * side(v) + side(w)


def image_rows():
    rows = [(y, z, b) for y in range(CY) for b in range(3) for z in range(CZ)]
    for y in (-1, CY):
        rows += [(y, z, b) for b in range(3) for z in range(CZ)] + [None] * 4
    for z in (-1, CZ):
        rows += [(y, z, b) for y in range(CY) for b in range(3)] + [None] * 4
    for y in (-1, CY):
        for z in (-1, CZ):
            rows += [(y, z, b) for b in range(3)] + [None]
    return rows


@functools.cache
def tables():
    rows = image_rows()
    index = np.full((128, 3 * PLANE), -1, np.int32)
    for r, row in enumerate(rows):
        if row is None:
            continue
        for p in range(3):
            for y in range(CY):
                for a in range(3):
                    for z in range(CZ):
                        oy, oz = row[0] - y, row[1] - z
                        if abs(oy) <= 1 and abs(oz) <= 1:
                            index[r, p * PLANE + y * 12 + a * 4 + z] = (3 * (oy + 1) + oz + 1) * 3 + row[2]
    widen = np.zeros((3, 27, 3 * PLANE), np.float32)
    for b in range(3):
        for p in range(3):
            for y in range(CY):
                for a in range(3):
                    for z in range(CZ):
                        widen[b, (2 - p) * 9 + a * 3 + b, p * PLANE + y * 12 + a * 4 + z] = 1
    pack = np.zeros((80, PLANE), np.float32)
    for r, row in enumerate(rows[48:]):
        if row is not None:
            y, z, a = row
            pack[r, (y % CY) * 12 + a * 4 + z % CZ] = 1
    regroup = np.zeros((128, 128), np.float32)
    for j in range(4):
        for x in range(CX):
            for b in range(4):
                regroup[j * 32 + x * 4 + b, x * 16 + j * 4 + b] = 1
    place = np.zeros((PLANE, 16), np.float32)
    for y in range(CY):
        for a in range(3):
            for z in range(CZ):
                place[y * 12 + a * 4 + z, y * CZ + z] = 1
    return index, widen, pack, regroup, place


def dot(a, b, precision=None):
    return jnp.dot(a, b, preferred_element_type=jnp.float32, precision=precision)


def contract(left, right):
    return lax.dot_general(left, right, (((0,), (0,)), ((), ())), preferred_element_type=jnp.float32)


def kernel(
    sizes,
    vec_ref, mat_ref, mod_ref, sten_ref, index_ref, widen_ref, pack_ref, regroup_ref, place_ref,
    out_ref,
    xp, pk, edge, cor, hx, hy, hz, hyz, hxy, hxz, hc, ic, iyz, icn, ie, stage, recv,
    halo_send, halo_recv, row_send, row_recv,
):
    n_x, n_y, n_z = sizes
    rows = VECS // n_z
    me = (lax.axis_index("gx"), lax.axis_index("gy"), lax.axis_index("gz"))

    def at(o):
        return tuple(lax.rem(me[i] + (o[i] + sizes[i]), sizes[i]) for i in range(3))

    line = [d for d in range(1, n_z) if d not in (1, n_z - 1)]
    barrier = pltpu.get_barrier_semaphore()
    for o in NEIGHBOURS:
        pl.semaphore_signal(barrier, inc=1, device_id=at(o), device_id_type=MESH)
    for d in line:
        pl.semaphore_signal(barrier, inc=1, device_id=at((0, 0, d)), device_id_type=MESH)

    mat = mat_ref[...]
    value = jnp.zeros(mat.shape, jnp.float32)
    for c in range(16):
        value = jnp.where(mat == c, mod_ref[c], value)
    root = jnp.sqrt(value)
    wide = jnp.concatenate([jnp.broadcast_to(root[:, x : x + 1], (16, VECS)) for x in range(CX)], axis=1)
    scale = dot(place_ref[...], wide, HIGHEST)
    empty = jnp.zeros((PLANE, VECS), jnp.bfloat16)
    for i in (0, 1, CX + 2, CX + 3):
        xp[i] = empty
    class_of = lax.broadcasted_iota(jnp.int32, (16, VECS), 0) // 4
    for x in range(CX):
        plane = (vec_ref[x].astype(jnp.float32) * scale[:, x * VECS : (x + 1) * VECS]).astype(jnp.bfloat16)
        xp[2 + x] = plane
        packed = dot(pack_ref[...], plane)
        for k in range(5):
            pk[k, x] = packed[16 * k : 16 * k + 16].astype(jnp.bfloat16)
        if x in (0, CX - 1):
            first = 0 if x == CX - 1 else 4
            for j in range(4):
                cor[first + j] = jnp.where(class_of == j, packed[64:80], 0.0).astype(jnp.bfloat16)
    dense = dot(regroup_ref[...], pk[4].reshape(CX * 16, VECS)).astype(jnp.bfloat16)
    for j in range(4):
        edge[j] = dense[32 * j : 32 * j + 32]

    pl.semaphore_wait(barrier, len(NEIGHBOURS) + len(line))

    def halo(r):
        xi = CX - 1 if r[0] < 0 else 0
        if r[1] == 0 and r[2] == 0:
            return xp.at[2 + xi], hx.at[side(r[0])]
        if r[0] == 0 and r[2] == 0:
            return pk.at[side(r[1])], hy.at[side(r[1])]
        if r[0] == 0 and r[1] == 0:
            return pk.at[2 + side(r[2])], hz.at[side(r[2])]
        if r[0] == 0:
            return edge.at[pair(r[1], r[2])], hyz.at[pair(r[1], r[2])]
        if r[2] == 0:
            return pk.at[side(r[1]), xi], hxy.at[pair(r[0], r[1])]
        if r[1] == 0:
            return pk.at[2 + side(r[2]), xi], hxz.at[pair(r[0], r[2])]
        k = 4 * side(r[0]) + pair(r[1], r[2])
        return cor.at[k], hc.at[k]

    copies = {}
    for r in sorted(NEIGHBOURS, key=lambda r: (r[1] == 0, -abs(r[0]) - abs(r[2]))):
        src, dst = halo(r)
        k = NEIGHBOURS.index(r)
        copies[r] = pltpu.make_async_remote_copy(
            src_ref=src, dst_ref=dst, send_sem=halo_send.at[k], recv_sem=halo_recv.at[k],
            device_id=at((-r[0], -r[1], -r[2])), device_id_type=MESH,
        )
        copies[r].start()

    index = index_ref[...]
    matrix = jnp.zeros(index.shape, jnp.float32)
    for b in range(3):
        table = dot(sten_ref[...], widen_ref[b], HIGHEST)
        for km in range(9):
            matrix = jnp.where(index == km * 3 + b, table[km : km + 1, :], matrix)
    high = matrix.astype(jnp.bfloat16)
    low = (matrix - high.astype(jnp.float32)).astype(jnp.bfloat16)
    for i in range(CX + 2):
        window = xp[i : i + 3].reshape(3 * PLANE, VECS)
        image = (dot(high, window) + dot(low, window)).astype(jnp.bfloat16)
        ic[i] = image[0:48]
        for k in range(4):
            iyz[k, i] = image[48 + 16 * k : 64 + 16 * k]
        icn[i] = image[112:128]
    dense = dot(regroup_ref[...], icn[1 : CX + 1].reshape(CX * 16, VECS)).astype(jnp.bfloat16)
    for j in range(4):
        ie[j] = dense[32 * j : 32 * j + 32]

    def operands(o):
        xi = 0 if o[0] < 0 else CX + 1
        inner = slice(1, CX + 1)
        if o == (0, 0, 0):
            return ic[inner].reshape(CX * PLANE, VECS), xp[2 : CX + 2].reshape(CX * PLANE, VECS)
        if o[1] == 0 and o[2] == 0:
            return ic[xi], hx[side(o[0])]
        if o[0] == 0 and o[2] == 0:
            k = side(o[1])
            return iyz[k, inner].reshape(CX * 16, VECS), hy[k].reshape(CX * 16, VECS)
        if o[0] == 0 and o[1] == 0:
            k = side(o[2])
            return iyz[2 + k, inner].reshape(CX * 16, VECS), hz[k].reshape(CX * 16, VECS)
        if o[0] == 0:
            k = pair(o[1], o[2])
            return ie[k], hyz[k]
        if o[2] == 0:
            return iyz[side(o[1]), xi], hxy[pair(o[0], o[1])]
        if o[1] == 0:
            return iyz[2 + side(o[2]), xi], hxz[pair(o[0], o[2])]
        return icn[xi], hc[4 * side(o[0]) + pair(o[1], o[2])]

    def inside(o):
        ok = None
        for i in range(3):
            if o[i] == 0:
                continue
            here = me[i] > 0 if o[i] < 0 else me[i] < sizes[i] - 1
            ok = here if ok is None else jnp.logical_and(ok, here)
        return ok

    def rows_copy(g, d, target, source):
        slots = pl.ds(STARTS[g], len(GROUPS[g]))
        return pltpu.make_async_remote_copy(
            src_ref=stage.at[target, slots], dst_ref=recv.at[source, slots],
            send_sem=row_send.at[g, d - 1], recv_sem=row_recv.at[g, d - 1],
            device_id=(me[0], me[1], target), device_id_type=MESH,
        )

    distances = sorted(range(1, n_z), key=lambda d: -min(d, n_z - d))
    for g, group in enumerate(GROUPS):
        for o in group:
            if o in copies:
                copies[o].wait_recv()
        for k, o in enumerate(group):
            left, right = operands(o)
            block = contract(left, right)
            if o != (0, 0, 0):
                block = jnp.where(inside(o), block, 0.0)
            stage[:, STARTS[g] + k] = block.reshape(n_z, rows, VECS).astype(jnp.bfloat16)
        for d in distances:
            rows_copy(g, d, lax.rem(me[2] + d, n_z), me[2]).start()

    def put(source, values):
        for k, o in enumerate(ORDER):
            out_ref.at[source][pl.ds(number(o), rows, stride=32), :] = values(k).astype(jnp.float32)

    put(me[2], lambda k: stage[me[2], k])
    for r in NEIGHBOURS:
        copies[r].wait_send()
    for d in reversed(distances):
        source = lax.rem(me[2] + n_z - d, n_z)
        for g in range(len(GROUPS)):
            rows_copy(g, d, lax.rem(me[2] + d, n_z), source).wait_recv()
        put(source, lambda k: recv[source, k])
    for d in distances:
        for g in range(len(GROUPS)):
            rows_copy(g, d, lax.rem(me[2] + d, n_z), me[2]).wait_send()


def body(sizes, deflation, material, moduli, stencil):
    n_z = sizes[2]
    rows = VECS // n_z
    vectors = jnp.transpose(deflation, (0, 1, 3, 2, 4)).reshape(CX, PLANE, VECS)
    classes = jnp.transpose(material, (1, 2, 0)).reshape(CY * CZ, CX)
    coupling = jnp.transpose(stencil.reshape(3, 9, 9), (1, 0, 2)).reshape(9, 27)
    index, widen, pack, regroup, place = tables()
    vmem = pl.BlockSpec(memory_space=pltpu.VMEM)
    b16 = jnp.bfloat16
    out = pl.pallas_call(
        functools.partial(kernel, sizes),
        out_shape=jax.ShapeDtypeStruct((n_z, rows * 32, VECS), jnp.float32),
        in_specs=[vmem, vmem, pl.BlockSpec(memory_space=pltpu.SMEM)] + [vmem] * 6,
        out_specs=vmem,
        scratch_shapes=[
            pltpu.VMEM((CX + 4, PLANE, VECS), b16),
            pltpu.VMEM((5, CX, 16, VECS), b16),
            pltpu.VMEM((4, 32, VECS), b16),
            pltpu.VMEM((8, 16, VECS), b16),
            pltpu.VMEM((2, PLANE, VECS), b16),
            pltpu.VMEM((2, CX, 16, VECS), b16),
            pltpu.VMEM((2, CX, 16, VECS), b16),
            pltpu.VMEM((4, 32, VECS), b16),
            pltpu.VMEM((4, 16, VECS), b16),
            pltpu.VMEM((4, 16, VECS), b16),
            pltpu.VMEM((8, 16, VECS), b16),
            pltpu.VMEM((CX + 2, PLANE, VECS), b16),
            pltpu.VMEM((4, CX + 2, 16, VECS), b16),
            pltpu.VMEM((CX + 2, 16, VECS), b16),
            pltpu.VMEM((4, 32, VECS), b16),
            pltpu.VMEM((n_z, 27, rows, VECS), b16),
            pltpu.VMEM((n_z, 27, rows, VECS), b16),
            pltpu.SemaphoreType.DMA((26,)),
            pltpu.SemaphoreType.DMA((26,)),
            pltpu.SemaphoreType.DMA((len(GROUPS), n_z - 1)),
            pltpu.SemaphoreType.DMA((len(GROUPS), n_z - 1)),
        ],
        compiler_params=pltpu.CompilerParams(collective_id=0, has_side_effects=True),
        name="coarse",
    )(vectors, classes, moduli, coupling, index, widen, jnp.asarray(pack, b16), jnp.asarray(regroup, b16), place)
    result = out.reshape(n_z, rows, 32, VECS)[:, :, :27]
    return jnp.transpose(result, (1, 0, 2, 3)).reshape(1, 1, rows, n_z, 27, VECS)


def solution(mesh):
    sizes = tuple(mesh.shape[name] for name in ("gx", "gy", "gz"))
    in_specs = (P("gx", "gy", "gz", None, None), P("gx", "gy", "gz"), P(), P())
    out_specs = P("gx", "gy", "gz", None, None, None)
    return jax.shard_map(
        functools.partial(body, sizes), mesh=mesh, in_specs=in_specs, out_specs=out_specs, check_vma=False
    )
```

profile of v0, /device:TPU:1, one launch (start us, length us, event | category | flops | bytes accessed | tf_op | source)
XLA Modules:
  0.0 61.8 jit_solution(7881234975789648283)
XLA Ops:
  0.0 0.8 %reshape.20 = f32[3,9,9]{1,0,2:T(4,128)S(1)} reshape(f32[27,3,3]{0,2,1:T(4,128)} %param.12) | data formatting | bytes 1944 | tf_op jit(solution)/shard_map/reshape | solution.py:266
  0.8 0.1 copy.10
  0.9 0.7 %reshape.21.sten_ref = f32[9,27]{1,0:T(8,128)} reshape(f32[9,3,9]{2,1,0:T(4,128)S(1)} %bitcast.18) | data formatting | bytes 1944 | tf_op jit(solution)/shard_map/reshape | solution.py:266
  1.6 56.0 %coarse.1 = f32[8,512,128]{2,1,0:T(8,128)} custom-call(bf16[8,48,128]{2,1,0:T(8,128)(2,1)} %bitcast.17, s32[16,8]{1,0:T(8,128)} %bitcast.19, f32[16]{0:T(128)} %mod_ref.1, f32[9,27]{1,0:T(8,128)} %reshape.21.sten_ref, s32[128,144]{1,0:T(8,128)} %constant.12.clone.index_ref, f32[3,27,144]{2,1,0:T(8,128)} %constant.13.clone.widen_ref, ...), custom_call_target="tpu_custom_call" | custom-call | tf_op jit(solution)/shard_map/coarse/pallas_call | solution.py:270
  57.6 4.2 %copy.14 = f32[8,16,27,128]{3,0,2,1:T(8,128)} copy(f32[8,16,27,128]{3,2,1,0:T(8,128)} %bitcast.16) | data formatting | bytes 3538944
where the time goes:
time: 62 us; the launch traced here: 61.8 us
  Pallas kernels  56 us (90%)
  local copies, waits for them, and re-layouts  5.75 us (9%)
    pallas_call x1, Pallas kernels, body(): pl.pallas_call(functools.partial(kernel, sizes), out_shape=jax.ShapeDtype...  56 us
    unnamed x1, local copies, waits for them, and re-layouts  4.18 us
    reshape x3, local copies, waits for them, and re-layouts, body(): coupling = jnp.transpose(stencil.reshape(3, 9, 9), (1, 0, 2)).reshape(9, 27)  1.57 us

commit v1 on v0

--- a/solution.py
+++ b/solution.py
@@ -62,12 +62,12 @@
                         if abs(oy) <= 1 and abs(oz) <= 1:
                             index[r, p * PLANE + y * 12 + a * 4 + z] = (3 * (oy + 1) + oz + 1) * 3 + row[2]
     widen = np.zeros((3, 27, 3 * PLANE), np.float32)
-    for b in range(3):
-        for p in range(3):
-            for y in range(CY):
-                for a in range(3):
-                    for z in range(CZ):
-                        widen[b, (2 - p) * 9 + a * 3 + b, p * PLANE + y * 12 + a * 4 + z] = 1
+    for n in range(27):
+        for y in range(CY):
+            for a in range(3):
+                for z in range(CZ):
+                    widen[a, n, (2 - n // 9) * PLANE + y * 12 + a * 4 + z] = 1
+    chosen = (np.arange(27)[None, :] % 9 == np.arange(16)[:, None]).astype(np.float32)
     pack = np.zeros((80, PLANE), np.float32)
     for r, row in enumerate(rows[48:]):
         if row is not None:
@@ -83,7 +83,7 @@
         for a in range(3):
             for z in range(CZ):
                 place[y * 12 + a * 4 + z, y * CZ + z] = 1
-    return index, widen, pack, regroup, place
+    return index, widen, chosen, pack, regroup, place
 
 
 def dot(a, b, precision=None):
@@ -96,12 +96,22 @@
 
 def kernel(
     sizes,
-    vec_ref, mat_ref, mod_ref, sten_ref, index_ref, widen_ref, pack_ref, regroup_ref, place_ref,
+    vec_in, mat_in, mod_in, sten_in, index_in, widen_in, chosen_in, pack_in, regroup_in, place_in,
     out_ref,
+    vec_ref, mat_ref, mod_ref, sten_ref, index_ref, widen_ref, chosen_ref, pack_ref, regroup_ref, place_ref, load_sem,
     xp, pk, edge, cor, hx, hy, hz, hyz, hxy, hxz, hc, ic, iyz, icn, ie, stage, recv,
     halo_send, halo_recv, row_send, row_recv,
 ):
-    n_x, n_y, n_z = sizes
+    loads = [
+        pltpu.make_async_copy(src, dst, load_sem.at[k])
+        for k, (src, dst) in enumerate([
+            (mat_in, mat_ref), (mod_in, mod_ref), (place_in, place_ref), (vec_in, vec_ref), (pack_in, pack_ref),
+            (regroup_in, regroup_ref), (sten_in, sten_ref), (index_in, index_ref), (widen_in, widen_ref), (chosen_in, chosen_ref),
+        ])
+    ]
+    for copy in loads:
+        copy.start()
+    n_z = sizes[2]
     rows = VECS // n_z
     me = (lax.axis_index("gx"), lax.axis_index("gy"), lax.axis_index("gz"))
 
@@ -115,6 +125,8 @@
     for d in line:
         pl.semaphore_signal(barrier, inc=1, device_id=at((0, 0, d)), device_id_type=MESH)
 
+    for copy in loads[:6]:
+        copy.wait()
     mat = mat_ref[...]
     value = jnp.zeros(mat.shape, jnp.float32)
     for c in range(16):
@@ -169,12 +181,19 @@
         )
         copies[r].start()
 
+    for copy in loads[6:]:
+        copy.wait()
     index = index_ref[...]
     matrix = jnp.zeros(index.shape, jnp.float32)
+    chosen = chosen_ref[...]
+    table = None
+    for a in range(3):
+        coupling = jnp.concatenate([chosen * sten_ref[a][b : b + 1, :] for b in range(3)], axis=0)
+        term = dot(coupling, widen_ref[a], HIGHEST)
+        table = term if table is None else table + term
     for b in range(3):
-        table = dot(sten_ref[...], widen_ref[b], HIGHEST)
         for km in range(9):
-            matrix = jnp.where(index == km * 3 + b, table[km : km + 1, :], matrix)
+            matrix = jnp.where(index == km * 3 + b, table[16 * b + km : 16 * b + km + 1, :], matrix)
     high = matrix.astype(jnp.bfloat16)
     low = (matrix - high.astype(jnp.float32)).astype(jnp.bfloat16)
     for i in range(CX + 2):
@@ -243,7 +262,7 @@
 
     def put(source, values):
         for k, o in enumerate(ORDER):
-            out_ref.at[source][pl.ds(number(o), rows, stride=32), :] = values(k).astype(jnp.float32)
+            out_ref[pl.ds(number(o) * n_z + source, rows, stride=27 * n_z), :] = values(k).astype(jnp.float32)
 
     put(me[2], lambda k: stage[me[2], k])
     for r in NEIGHBOURS:
@@ -263,16 +282,21 @@
     rows = VECS // n_z
     vectors = jnp.transpose(deflation, (0, 1, 3, 2, 4)).reshape(CX, PLANE, VECS)
     classes = jnp.transpose(material, (1, 2, 0)).reshape(CY * CZ, CX)
-    coupling = jnp.transpose(stencil.reshape(3, 9, 9), (1, 0, 2)).reshape(9, 27)
-    index, widen, pack, regroup, place = tables()
-    vmem = pl.BlockSpec(memory_space=pltpu.VMEM)
+    coupling = jnp.transpose(stencil, (1, 2, 0))
+    index, widen, chosen, pack, regroup, place = tables()
     b16 = jnp.bfloat16
+    operands = (
+        vectors, classes, moduli, coupling, index, widen, chosen,
+        jnp.asarray(pack, b16), jnp.asarray(regroup, b16), place,
+    )
+    spaces = [pltpu.SMEM if k == 2 else pltpu.VMEM for k in range(len(operands))]
     out = pl.pallas_call(
         functools.partial(kernel, sizes),
-        out_shape=jax.ShapeDtypeStruct((n_z, rows * 32, VECS), jnp.float32),
-        in_specs=[vmem, vmem, pl.BlockSpec(memory_space=pltpu.SMEM)] + [vmem] * 6,
-        out_specs=vmem,
-        scratch_shapes=[
+        out_shape=jax.ShapeDtypeStruct((rows * 27 * n_z, VECS), jnp.float32),
+        in_specs=[pl.BlockSpec(memory_space=pltpu.HBM)] * len(operands),
+        out_specs=pl.BlockSpec(memory_space=pltpu.VMEM),
+        scratch_shapes=[space(v.shape, v.dtype) for space, v in zip(spaces, operands)] + [
+            pltpu.SemaphoreType.DMA((len(operands),)),
             pltpu.VMEM((CX + 4, PLANE, VECS), b16),
             pltpu.VMEM((5, CX, 16, VECS), b16),
             pltpu.VMEM((4, 32, VECS), b16),
@@ -295,11 +319,10 @@
             pltpu.SemaphoreType.DMA((len(GROUPS), n_z - 1)),
             pltpu.SemaphoreType.DMA((len(GROUPS), n_z - 1)),
         ],
-        compiler_params=pltpu.CompilerParams(collective_id=0, has_side_effects=True),
+        compiler_params=pltpu.CompilerParams(collective_id=0, has_side_effects=True, vmem_limit_bytes=24 * 2**20),
         name="coarse",
-    )(vectors, classes, moduli, coupling, index, widen, jnp.asarray(pack, b16), jnp.asarray(regroup, b16), place)
-    result = out.reshape(n_z, rows, 32, VECS)[:, :, :27]
-    return jnp.transpose(result, (1, 0, 2, 3)).reshape(1, 1, rows, n_z, 27, VECS)
+    )(*[pltpu.with_memory_space_constraint(v, pltpu.HBM) for v in operands])
+    return jnp.transpose(out.reshape(1, 1, rows, 27, n_z, VECS), (0, 1, 2, 4, 3, 5))
 
 
 def solution(mesh):

time: 62 us -> 54.4 us (0.88)
  local copies, waits for them, and re-layouts: 5.75 us -> 1.21 us
  Pallas kernels: 56 us -> 53 us
    pallas_call x1, Pallas kernels: 56 us -> 53 us  [body(): pl.pallas_call(functools.partial(kernel, sizes), out_shape=jax.ShapeDtype...]
    unnamed x1, local copies, waits for them, and re-layouts: 4.18 us -> 1.21 us
    reshape x3 -> x0, local copies, waits for them, and re-layouts: 1.57 us -> none  [body(): coupling = jnp.transpose(stencil.reshape(3, 9, 9), (1, 0, 2)).reshape(9, 27)]
where the time goes in v1:
time: 54.4 us; the launch traced here: 54.2 us
  Pallas kernels  53 us (97%)
  local copies, waits for them, and re-layouts  1.21 us (2%)
    pallas_call x1, Pallas kernels, body(): pl.pallas_call(functools.partial(kernel, sizes), out_shape=jax.ShapeDtype...  53 us
    unnamed x1, local copies, waits for them, and re-layouts  1.21 us

profile of v1, /device:TPU:1, one launch (start us, length us, event | category | flops | bytes accessed | tf_op | source)
XLA Modules:
  0.0 54.2 jit_solution(352418978852754334)
XLA Ops:
  0.0 53.0 %coarse.1 = f32[3456,128]{1,0:T(8,128)S(1)} custom-call(bf16[8,48,128]{2,1,0:T(8,128)(2,1)} %bitcast.11, s32[16,8]{1,0:T(8,128)} %bitcast.12, f32[16]{0:T(128)} %mod_in.1, f32[3,3,27]{2,1,0:T(4,128)} %bitcast.13, s32[128,144]{1,0:T(8,128)} %constant.14.clone.index_in, f32[3,27,144]{2,1,0:T(8,128)} %constant.15.clone.widen_in, ...), custom_call_target="tpu_custom_call" | custom-call | tf_op jit(solution)/shard_map/coarse/pallas_call | solution.py:293
  53.0 1.2 %copy.12 = f32[1,1,16,8,27,128]{5,3,4,2,1,0:T(8,128)} copy(f32[1,1,16,8,27,128]{5,3,4,2,1,0:T(8,128)S(1)} %bitcast.10) | data formatting | bytes 3538944

commit v2 on v1

--- a/solution.py
+++ b/solution.py
@@ -13,14 +13,16 @@
 CX, CY, CZ, VECS = 8, 4, 4, 128
 PLANE = CY * 3 * CZ
 OFFSETS = [(i, j, k) for i in (-1, 0, 1) for j in (-1, 0, 1) for k in (-1, 0, 1)]
-NEIGHBOURS = [o for o in OFFSETS if o != (0, 0, 0)]
+CROSS = [(i, j) for i in (-1, 1) for j in (-1, 1)]
+NEIGHBOURS = [o for o in OFFSETS if o != (0, 0, 0) and 0 in o]
 GROUPS = (
     [(0, 0, 0)],
     [o for o in NEIGHBOURS if o[1] == 0],
-    [o for o in NEIGHBOURS if o[1] != 0],
+    [o for o in NEIGHBOURS if o[0] == 0 and o[1] != 0],
 )
 ORDER = [o for g in GROUPS for o in g]
-STARTS = [sum(len(g) for g in GROUPS[:i]) for i in range(len(GROUPS))]
+SLOTS = (slice(0, 2), slice(2, 10), slice(10, 16))
+PLACES = [0] + list(range(2, 16))
 
 
 def number(o):
@@ -83,7 +85,14 @@
         for a in range(3):
             for z in range(CZ):
                 place[y * 12 + a * 4 + z, y * CZ + z] = 1
-    return index, widen, chosen, pack, regroup, place
+    choose = np.zeros((128, 12, 8, 16), np.float32)
+    for g, (_, y) in enumerate(CROSS):
+        for a in range(3):
+            for z in range(CZ):
+                choose[g * 32 + a * 4 + z, 3 * g + 1, :, a * 4 + z] = 1
+            choose[g * 32 + 16 + pair(y, -1) * 4 + a, 3 * g, :, a * 4 + CZ - 1] = 1
+            choose[g * 32 + 16 + pair(y, 1) * 4 + a, 3 * g + 2, :, a * 4] = 1
+    return index, widen, chosen, pack, regroup, place, np.eye(128, dtype=np.float32), choose.reshape(128, 1536)
 
 
 def dot(a, b, precision=None):
@@ -96,10 +105,10 @@
 
 def kernel(
     sizes,
-    vec_in, mat_in, mod_in, sten_in, index_in, widen_in, chosen_in, pack_in, regroup_in, place_in,
+    vec_in, mat_in, mod_in, sten_in, index_in, widen_in, chosen_in, pack_in, regroup_in, place_in, eye_in, choose_in,
     out_ref,
-    vec_ref, mat_ref, mod_ref, sten_ref, index_ref, widen_ref, chosen_ref, pack_ref, regroup_ref, place_ref, load_sem,
-    xp, pk, edge, cor, hx, hy, hz, hyz, hxy, hxz, hc, ic, iyz, icn, ie, stage, recv,
+    vec_ref, mat_ref, mod_ref, sten_ref, index_ref, widen_ref, chosen_ref, pack_ref, regroup_ref, place_ref, eye_ref, choose_ref, load_sem,
+    xp, pk, edge, hx, hy, hz, hyz, hxy, hxz, ic, iyz, icn, ie, stage, recv, cells,
     halo_send, halo_recv, row_send, row_recv,
 ):
     loads = [
@@ -107,6 +116,7 @@
         for k, (src, dst) in enumerate([
             (mat_in, mat_ref), (mod_in, mod_ref), (place_in, place_ref), (vec_in, vec_ref), (pack_in, pack_ref),
             (regroup_in, regroup_ref), (sten_in, sten_ref), (index_in, index_ref), (widen_in, widen_ref), (chosen_in, chosen_ref),
+            (eye_in, eye_ref), (choose_in, choose_ref),
         ])
     ]
     for copy in loads:
@@ -137,17 +147,12 @@
     empty = jnp.zeros((PLANE, VECS), jnp.bfloat16)
     for i in (0, 1, CX + 2, CX + 3):
         xp[i] = empty
-    class_of = lax.broadcasted_iota(jnp.int32, (16, VECS), 0) // 4
     for x in range(CX):
         plane = (vec_ref[x].astype(jnp.float32) * scale[:, x * VECS : (x + 1) * VECS]).astype(jnp.bfloat16)
         xp[2 + x] = plane
         packed = dot(pack_ref[...], plane)
         for k in range(5):
             pk[k, x] = packed[16 * k : 16 * k + 16].astype(jnp.bfloat16)
-        if x in (0, CX - 1):
-            first = 0 if x == CX - 1 else 4
-            for j in range(4):
-                cor[first + j] = jnp.where(class_of == j, packed[64:80], 0.0).astype(jnp.bfloat16)
     dense = dot(regroup_ref[...], pk[4].reshape(CX * 16, VECS)).astype(jnp.bfloat16)
     for j in range(4):
         edge[j] = dense[32 * j : 32 * j + 32]
@@ -166,10 +171,7 @@
             return edge.at[pair(r[1], r[2])], hyz.at[pair(r[1], r[2])]
         if r[2] == 0:
             return pk.at[side(r[1]), xi], hxy.at[pair(r[0], r[1])]
-        if r[1] == 0:
-            return pk.at[2 + side(r[2]), xi], hxz.at[pair(r[0], r[2])]
-        k = 4 * side(r[0]) + pair(r[1], r[2])
-        return cor.at[k], hc.at[k]
+        return pk.at[2 + side(r[2]), xi], hxz.at[pair(r[0], r[2])]
 
     copies = {}
     for r in sorted(NEIGHBOURS, key=lambda r: (r[1] == 0, -abs(r[0]) - abs(r[2]))):
@@ -223,11 +225,7 @@
         if o[0] == 0:
             k = pair(o[1], o[2])
             return ie[k], hyz[k]
-        if o[2] == 0:
-            return iyz[side(o[1]), xi], hxy[pair(o[0], o[1])]
-        if o[1] == 0:
-            return iyz[2 + side(o[2]), xi], hxz[pair(o[0], o[2])]
-        return icn[xi], hc[4 * side(o[0]) + pair(o[1], o[2])]
+        return iyz[2 + side(o[2]), xi], hxz[pair(o[0], o[2])]
 
     def inside(o):
         ok = None
@@ -239,41 +237,79 @@
         return ok
 
     def rows_copy(g, d, target, source):
-        slots = pl.ds(STARTS[g], len(GROUPS[g]))
+        if g == len(GROUPS):
+            src, dst = hxy, cells.at[source]
+        else:
+            slots = pl.ds(SLOTS[g].start, SLOTS[g].stop - SLOTS[g].start)
+            src, dst = stage.at[target, slots], recv.at[source, slots]
         return pltpu.make_async_remote_copy(
-            src_ref=stage.at[target, slots], dst_ref=recv.at[source, slots],
-            send_sem=row_send.at[g, d - 1], recv_sem=row_recv.at[g, d - 1],
+            src_ref=src, dst_ref=dst, send_sem=row_send.at[g, d - 1], recv_sem=row_recv.at[g, d - 1],
             device_id=(me[0], me[1], target), device_id_type=MESH,
         )
 
     distances = sorted(range(1, n_z), key=lambda d: -min(d, n_z - d))
+
+    def send(g):
+        for d in distances:
+            rows_copy(g, d, lax.rem(me[2] + d, n_z), me[2]).start()
+
+    def receive(g, d):
+        rows_copy(g, d, lax.rem(me[2] + d, n_z), lax.rem(me[2] + n_z - d, n_z)).wait_recv()
+
+    few = [v for x, y in CROSS for v in (iyz[side(y), (CX + 1) * side(x)], icn[(CX + 1) * side(x)])]
+    few = contract(jnp.concatenate(few, axis=0), eye_ref[...]).reshape(n_z, rows, VECS).astype(jnp.bfloat16)
+    stage[:, 1] = few
     for g, group in enumerate(GROUPS):
+        if g == 2:
+            for x, y in CROSS:
+                copies[x, y, 0].wait_recv()
+            send(len(GROUPS))
+            cells[me[2]] = hxy[...]
         for o in group:
             if o in copies:
                 copies[o].wait_recv()
-        for k, o in enumerate(group):
+        for o in group:
             left, right = operands(o)
             block = contract(left, right)
             if o != (0, 0, 0):
                 block = jnp.where(inside(o), block, 0.0)
-            stage[:, STARTS[g] + k] = block.reshape(n_z, rows, VECS).astype(jnp.bfloat16)
-        for d in distances:
-            rows_copy(g, d, lax.rem(me[2] + d, n_z), me[2]).start()
-
-    def put(source, values):
-        for k, o in enumerate(ORDER):
-            out_ref[pl.ds(number(o) * n_z + source, rows, stride=27 * n_z), :] = values(k).astype(jnp.float32)
-
-    put(me[2], lambda k: stage[me[2], k])
+            stage[:, PLACES[ORDER.index(o)]] = block.reshape(n_z, rows, VECS).astype(jnp.bfloat16)
+        send(g)
+
+    def put(o, source, value):
+        out_ref[pl.ds(number(o) * n_z + source, rows, stride=27 * n_z), :] = value
+
+    for o, k in zip(ORDER, PLACES):
+        put(o, me[2], stage[me[2], k].astype(jnp.float32))
+    recv[me[2], 1] = stage[me[2], 1]
     for r in NEIGHBOURS:
         copies[r].wait_send()
+
+    for d in distances:
+        receive(0, d)
+        receive(len(GROUPS), d)
+    few = recv[:, 1].reshape(VECS, VECS)
+    from_cell = lax.broadcasted_iota(jnp.int32, (VECS, 16 * n_z), 0) // rows
+    to_cell = lax.broadcasted_iota(jnp.int32, (VECS, 16 * n_z), 1) // 16
+    for i, (x, y) in enumerate(CROSS):
+        right = cells[:, i].reshape(n_z * 16, VECS)
+        ok = inside((x, y, 0))
+        for z in (-1, 0, 1):
+            start = (3 * i + z + 1) * 128
+            left = dot(few, choose_ref[:, start : start + 16 * n_z])
+            left = jnp.where(from_cell + z == to_cell, left, 0.0).astype(jnp.bfloat16)
+            block = jnp.where(ok, dot(left, right), 0.0)
+            for source in range(n_z):
+                put((x, y, z), source, block[source * rows : (source + 1) * rows])
+
     for d in reversed(distances):
+        receive(1, d)
+        receive(2, d)
         source = lax.rem(me[2] + n_z - d, n_z)
-        for g in range(len(GROUPS)):
-            rows_copy(g, d, lax.rem(me[2] + d, n_z), source).wait_recv()
-        put(source, lambda k: recv[source, k])
+        for o, k in zip(ORDER, PLACES):
+            put(o, source, recv[source, k].astype(jnp.float32))
     for d in distances:
-        for g in range(len(GROUPS)):
+        for g in range(len(GROUPS) + 1):
             rows_copy(g, d, lax.rem(me[2] + d, n_z), me[2]).wait_send()
 
 
@@ -283,11 +319,11 @@
     vectors = jnp.transpose(deflation, (0, 1, 3, 2, 4)).reshape(CX, PLANE, VECS)
     classes = jnp.transpose(material, (1, 2, 0)).reshape(CY * CZ, CX)
     coupling = jnp.transpose(stencil, (1, 2, 0))
-    index, widen, chosen, pack, regroup, place = tables()
+    index, widen, chosen, pack, regroup, place, eye, choose = tables()
     b16 = jnp.bfloat16
     operands = (
         vectors, classes, moduli, coupling, index, widen, chosen,
-        jnp.asarray(pack, b16), jnp.asarray(regroup, b16), place,
+        jnp.asarray(pack, b16), jnp.asarray(regroup, b16), place, jnp.asarray(eye, b16), jnp.asarray(choose, b16),
     )
     spaces = [pltpu.SMEM if k == 2 else pltpu.VMEM for k in range(len(operands))]
     out = pl.pallas_call(
@@ -300,24 +336,23 @@
             pltpu.VMEM((CX + 4, PLANE, VECS), b16),
             pltpu.VMEM((5, CX, 16, VECS), b16),
             pltpu.VMEM((4, 32, VECS), b16),
-            pltpu.VMEM((8, 16, VECS), b16),
             pltpu.VMEM((2, PLANE, VECS), b16),
             pltpu.VMEM((2, CX, 16, VECS), b16),
             pltpu.VMEM((2, CX, 16, VECS), b16),
             pltpu.VMEM((4, 32, VECS), b16),
             pltpu.VMEM((4, 16, VECS), b16),
             pltpu.VMEM((4, 16, VECS), b16),
-            pltpu.VMEM((8, 16, VECS), b16),
             pltpu.VMEM((CX + 2, PLANE, VECS), b16),
             pltpu.VMEM((4, CX + 2, 16, VECS), b16),
             pltpu.VMEM((CX + 2, 16, VECS), b16),
             pltpu.VMEM((4, 32, VECS), b16),
-            pltpu.VMEM((n_z, 27, rows, VECS), b16),
-            pltpu.VMEM((n_z, 27, rows, VECS), b16),
-            pltpu.SemaphoreType.DMA((26,)),
-            pltpu.SemaphoreType.DMA((26,)),
-            pltpu.SemaphoreType.DMA((len(GROUPS), n_z - 1)),
-            pltpu.SemaphoreType.DMA((len(GROUPS), n_z - 1)),
+            pltpu.VMEM((n_z, 16, rows, VECS), b16),
+            pltpu.VMEM((n_z, 16, rows, VECS), b16),
+            pltpu.VMEM((n_z, 4, 16, VECS), b16),
+            pltpu.SemaphoreType.DMA((len(NEIGHBOURS),)),
+            pltpu.SemaphoreType.DMA((len(NEIGHBOURS),)),
+            pltpu.SemaphoreType.DMA((len(GROUPS) + 1, n_z - 1)),
+            pltpu.SemaphoreType.DMA((len(GROUPS) + 1, n_z - 1)),
         ],
         compiler_params=pltpu.CompilerParams(collective_id=0, has_side_effects=True, vmem_limit_bytes=24 * 2**20),
         name="coarse",

time: 54.4 us -> 47.8 us (0.88)
  Pallas kernels: 53 us -> 46.4 us
    pallas_call x1, Pallas kernels: 53 us -> 46.4 us  [body(): pl.pallas_call(functools.partial(kernel, sizes), out_shape=jax.ShapeDtype...]
where the time goes in v2:
time: 47.8 us; the launch traced here: 47.6 us
  Pallas kernels  46.4 us (97%)
  local copies, waits for them, and re-layouts  1.21 us (3%)
    pallas_call x1, Pallas kernels, body(): pl.pallas_call(functools.partial(kernel, sizes), out_shape=jax.ShapeDtype...  46.4 us
    unnamed x1, local copies, waits for them, and re-layouts  1.21 us

profile of v2, /device:TPU:1, one launch (start us, length us, event | category | flops | bytes accessed | tf_op | source)
XLA Modules:
  0.0 47.6 jit_solution(15501683815207715724)
XLA Ops:
  0.0 46.4 %coarse.1 = f32[3456,128]{1,0:T(8,128)S(1)} custom-call(bf16[8,48,128]{2,1,0:T(8,128)(2,1)} %bitcast.11, s32[16,8]{1,0:T(8,128)} %bitcast.12, f32[16]{0:T(128)} %mod_in.1, f32[3,3,27]{2,1,0:T(4,128)} %bitcast.13, s32[128,144]{1,0:T(8,128)} %constant.20.clone.index_in, f32[3,27,144]{2,1,0:T(8,128)} %constant.21.clone.widen_in, ...), custom_call_target="tpu_custom_call" | custom-call | tf_op jit(solution)/shard_map/coarse/pallas_call | solution.py:329
  46.4 1.2 %copy.14 = f32[1,1,16,8,27,128]{5,3,4,2,1,0:T(8,128)} copy(f32[1,1,16,8,27,128]{5,3,4,2,1,0:T(8,128)S(1)} %bitcast.10) | data formatting | bytes 3538944

commit v3 on v2

--- a/solution.py
+++ b/solution.py
@@ -128,11 +128,27 @@
     def at(o):
         return tuple(lax.rem(me[i] + (o[i] + sizes[i]), sizes[i]) for i in range(3))
 
-    line = [d for d in range(1, n_z) if d not in (1, n_z - 1)]
+    def inside(o):
+        ok = None
+        for i in range(3):
+            if o[i] == 0:
+                continue
+            here = me[i] > 0 if o[i] < 0 else me[i] < sizes[i] - 1
+            ok = here if ok is None else jnp.logical_and(ok, here)
+        return ok
+
     barrier = pltpu.get_barrier_semaphore()
+    present = jnp.int32(n_z - 1)
     for o in NEIGHBOURS:
-        pl.semaphore_signal(barrier, inc=1, device_id=at(o), device_id_type=MESH)
-    for d in line:
+        if o[:2] == (0, 0):
+            continue
+        present = present + inside(o).astype(jnp.int32)
+
+        @pl.when(inside(o))
+        def _():
+            pl.semaphore_signal(barrier, inc=1, device_id=at(o), device_id_type=MESH)
+
+    for d in range(1, n_z):
         pl.semaphore_signal(barrier, inc=1, device_id=at((0, 0, d)), device_id_type=MESH)
 
     for copy in loads[:6]:
@@ -157,7 +173,7 @@
     for j in range(4):
         edge[j] = dense[32 * j : 32 * j + 32]
 
-    pl.semaphore_wait(barrier, len(NEIGHBOURS) + len(line))
+    pl.semaphore_wait(barrier, present)
 
     def halo(r):
         xi = CX - 1 if r[0] < 0 else 0
@@ -181,7 +197,10 @@
             src_ref=src, dst_ref=dst, send_sem=halo_send.at[k], recv_sem=halo_recv.at[k],
             device_id=at((-r[0], -r[1], -r[2])), device_id_type=MESH,
         )
-        copies[r].start()
+
+        @pl.when(inside((-r[0], -r[1], -r[2])))
+        def _():
+            copies[r].start()
 
     for copy in loads[6:]:
         copy.wait()
@@ -227,15 +246,6 @@
             return ie[k], hyz[k]
         return iyz[2 + side(o[2]), xi], hxz[pair(o[0], o[2])]
 
-    def inside(o):
-        ok = None
-        for i in range(3):
-            if o[i] == 0:
-                continue
-            here = me[i] > 0 if o[i] < 0 else me[i] < sizes[i] - 1
-            ok = here if ok is None else jnp.logical_and(ok, here)
-        return ok
-
     def rows_copy(g, d, target, source):
         if g == len(GROUPS):
             src, dst = hxy, cells.at[source]
@@ -247,6 +257,11 @@
             device_id=(me[0], me[1], target), device_id_type=MESH,
         )
 
+    def arrive(o):
+        @pl.when(inside(o))
+        def _():
+            copies[o].wait_recv()
+
     distances = sorted(range(1, n_z), key=lambda d: -min(d, n_z - d))
 
     def send(g):
@@ -262,12 +277,12 @@
     for g, group in enumerate(GROUPS):
         if g == 2:
             for x, y in CROSS:
-                copies[x, y, 0].wait_recv()
+                arrive((x, y, 0))
             send(len(GROUPS))
             cells[me[2]] = hxy[...]
         for o in group:
             if o in copies:
-                copies[o].wait_recv()
+                arrive(o)
         for o in group:
             left, right = operands(o)
             block = contract(left, right)
@@ -283,7 +298,10 @@
         put(o, me[2], stage[me[2], k].astype(jnp.float32))
     recv[me[2], 1] = stage[me[2], 1]
     for r in NEIGHBOURS:
-        copies[r].wait_send()
+
+        @pl.when(inside((-r[0], -r[1], -r[2])))
+        def _():
+            copies[r].wait_send()
 
     for d in distances:
         receive(0, d)

time: 47.8 us -> 36.6 us (0.77)
  Pallas kernels: 46.4 us -> 35.3 us
    pallas_call x1, Pallas kernels: 46.4 us -> 35.3 us  [body(): pl.pallas_call(functools.partial(kernel, sizes), out_shape=jax.ShapeDtype...]
where the time goes in v3:
time: 36.6 us; the launch traced here: 36.5 us
  Pallas kernels  35.3 us (96%)
  local copies, waits for them, and re-layouts  1.21 us (3%)
    pallas_call x1, Pallas kernels, body(): pl.pallas_call(functools.partial(kernel, sizes), out_shape=jax.ShapeDtype...  35.3 us
    unnamed x1, local copies, waits for them, and re-layouts  1.21 us

profile of v3, /device:TPU:1, one launch (start us, length us, event | category | flops | bytes accessed | tf_op | source)
XLA Modules:
  0.0 36.5 jit_solution(6222849148629593589)
XLA Ops:
  0.0 35.3 %coarse.1 = f32[3456,128]{1,0:T(8,128)S(1)} custom-call(bf16[8,48,128]{2,1,0:T(8,128)(2,1)} %bitcast.11, s32[16,8]{1,0:T(8,128)} %bitcast.12, f32[16]{0:T(128)} %mod_in.1, f32[3,3,27]{2,1,0:T(4,128)} %bitcast.13, s32[128,144]{1,0:T(8,128)} %constant.20.clone.index_in, f32[3,27,144]{2,1,0:T(8,128)} %constant.21.clone.widen_in, ...), custom_call_target="tpu_custom_call" | custom-call | tf_op jit(solution)/shard_map/coarse/pallas_call | solution.py:347
  35.3 1.2 %copy.14 = f32[1,1,16,8,27,128]{5,3,4,2,1,0:T(8,128)} copy(f32[1,1,16,8,27,128]{5,3,4,2,1,0:T(8,128)S(1)} %bitcast.10) | data formatting | bytes 3538944

commit v4 on v3

--- a/solution.py
+++ b/solution.py
@@ -109,7 +109,7 @@
     out_ref,
     vec_ref, mat_ref, mod_ref, sten_ref, index_ref, widen_ref, chosen_ref, pack_ref, regroup_ref, place_ref, eye_ref, choose_ref, load_sem,
     xp, pk, edge, hx, hy, hz, hyz, hxy, hxz, ic, iyz, icn, ie, stage, recv, cells,
-    halo_send, halo_recv, row_send, row_recv,
+    halo_send, halo_recv, row_send, row_recv, ready, origin_ready,
 ):
     loads = [
         pltpu.make_async_copy(src, dst, load_sem.at[k])
@@ -137,19 +137,36 @@
             ok = here if ok is None else jnp.logical_and(ok, here)
         return ok
 
+    both, negate = jnp.logical_and, jnp.logical_not
+    origin_line = both(me[0] == 0, me[1] == 0)
+    origin = both(origin_line, me[2] == 0)
+
+    def to_origin(o):
+        if max(o) > 0:
+            return None
+        return both(both(me[0] + o[0] == 0, me[1] + o[1] == 0), me[2] + o[2] == 0)
+
+    def except_origin(o):
+        return inside(o) if max(o) > 0 else both(inside(o), negate(to_origin(o)))
+
+    beside = [o for o in NEIGHBOURS if o[:2] != (0, 0)]
     barrier = pltpu.get_barrier_semaphore()
-    present = jnp.int32(n_z - 1)
-    for o in NEIGHBOURS:
-        if o[:2] == (0, 0):
+    expected = jnp.int32(n_z - 1) - both(origin_line, negate(origin)).astype(jnp.int32)
+    for o in beside:
+        awaited = both(inside(o), origin) if o[1] > 0 else except_origin(o)
+        expected = expected + awaited.astype(jnp.int32)
+        told = inside(o) if o[1] >= 0 else to_origin(o)
+        if told is None:
             continue
-        present = present + inside(o).astype(jnp.int32)
-
-        @pl.when(inside(o))
+
+        @pl.when(both(told, negate(origin)))
         def _():
             pl.semaphore_signal(barrier, inc=1, device_id=at(o), device_id_type=MESH)
 
-    for d in range(1, n_z):
-        pl.semaphore_signal(barrier, inc=1, device_id=at((0, 0, d)), device_id_type=MESH)
+    @pl.when(negate(origin))
+    def _():
+        for d in range(1, n_z):
+            pl.semaphore_signal(barrier, inc=1, device_id=at((0, 0, d)), device_id_type=MESH)
 
     for copy in loads[:6]:
         copy.wait()
@@ -173,35 +190,6 @@
     for j in range(4):
         edge[j] = dense[32 * j : 32 * j + 32]
 
-    pl.semaphore_wait(barrier, present)
-
-    def halo(r):
-        xi = CX - 1 if r[0] < 0 else 0
-        if r[1] == 0 and r[2] == 0:
-            return xp.at[2 + xi], hx.at[side(r[0])]
-        if r[0] == 0 and r[2] == 0:
-            return pk.at[side(r[1])], hy.at[side(r[1])]
-        if r[0] == 0 and r[1] == 0:
-            return pk.at[2 + side(r[2])], hz.at[side(r[2])]
-        if r[0] == 0:
-            return edge.at[pair(r[1], r[2])], hyz.at[pair(r[1], r[2])]
-        if r[2] == 0:
-            return pk.at[side(r[1]), xi], hxy.at[pair(r[0], r[1])]
-        return pk.at[2 + side(r[2]), xi], hxz.at[pair(r[0], r[2])]
-
-    copies = {}
-    for r in sorted(NEIGHBOURS, key=lambda r: (r[1] == 0, -abs(r[0]) - abs(r[2]))):
-        src, dst = halo(r)
-        k = NEIGHBOURS.index(r)
-        copies[r] = pltpu.make_async_remote_copy(
-            src_ref=src, dst_ref=dst, send_sem=halo_send.at[k], recv_sem=halo_recv.at[k],
-            device_id=at((-r[0], -r[1], -r[2])), device_id_type=MESH,
-        )
-
-        @pl.when(inside((-r[0], -r[1], -r[2])))
-        def _():
-            copies[r].start()
-
     for copy in loads[6:]:
         copy.wait()
     index = index_ref[...]
@@ -217,6 +205,72 @@
             matrix = jnp.where(index == km * 3 + b, table[16 * b + km : 16 * b + km + 1, :], matrix)
     high = matrix.astype(jnp.bfloat16)
     low = (matrix - high.astype(jnp.float32)).astype(jnp.bfloat16)
+    pl.semaphore_wait(barrier, expected)
+    for o in beside:
+        if o[1] < 0:
+
+            @pl.when(except_origin(o))
+            def _():
+                pl.semaphore_signal(ready, inc=1, device_id=at(o), device_id_type=MESH)
+
+    @pl.when(origin)
+    def _():
+        for o in beside:
+            if min(o) >= 0:
+                pl.semaphore_signal(origin_ready, inc=1, device_id=at(o), device_id_type=MESH)
+        for d in range(1, n_z):
+            pl.semaphore_signal(origin_ready, inc=1, device_id=at((0, 0, d)), device_id_type=MESH)
+
+    def halo(r):
+        xi = CX - 1 if r[0] < 0 else 0
+        if r[1] == 0 and r[2] == 0:
+            return xp.at[2 + xi], hx.at[side(r[0])]
+        if r[0] == 0 and r[2] == 0:
+            return pk.at[side(r[1])], hy.at[side(r[1])]
+        if r[0] == 0 and r[1] == 0:
+            return pk.at[2 + side(r[2])], hz.at[side(r[2])]
+        if r[0] == 0:
+            return edge.at[pair(r[1], r[2])], hyz.at[pair(r[1], r[2])]
+        if r[2] == 0:
+            return pk.at[side(r[1]), xi], hxy.at[pair(r[0], r[1])]
+        return pk.at[2 + side(r[2]), xi], hxz.at[pair(r[0], r[2])]
+
+    copies = {}
+    for r in sorted(NEIGHBOURS, key=lambda r: (r[1] == 0, -abs(r[0]) - abs(r[2]))):
+        src, dst = halo(r)
+        k = NEIGHBOURS.index(r)
+        copies[r] = pltpu.make_async_remote_copy(
+            src_ref=src, dst_ref=dst, send_sem=halo_send.at[k], recv_sem=halo_recv.at[k],
+            device_id=at((-r[0], -r[1], -r[2])), device_id_type=MESH,
+        )
+        o = (-r[0], -r[1], -r[2])
+
+        @pl.when(both(inside(o), origin) if o[1] > 0 else except_origin(o))
+        def _():
+            copies[r].start()
+
+    def to_the_origin(level):
+        for r in NEIGHBOURS:
+            if min(r) >= 0 and r[1] == level:
+
+                @pl.when(to_origin((-r[0], -r[1], -r[2])))
+                def _():
+                    pl.semaphore_wait(origin_ready, 1)
+                    copies[r].start()
+
+    def up():
+        above = [o for o in beside if o[1] > 0]
+
+        @pl.when(both(inside((0, 1, 0)), negate(origin)))
+        def _():
+            pl.semaphore_wait(ready, sum(inside(o).astype(jnp.int32) for o in above))
+
+        for o in above:
+
+            @pl.when(both(inside(o), negate(origin)))
+            def _():
+                copies[-o[0], -o[1], -o[2]].start()
+
     for i in range(CX + 2):
         window = xp[i : i + 3].reshape(3 * PLANE, VECS)
         image = (dot(high, window) + dot(low, window)).astype(jnp.bfloat16)
@@ -266,7 +320,11 @@
 
     def send(g):
         for d in distances:
-            rows_copy(g, d, lax.rem(me[2] + d, n_z), me[2]).start()
+            target = lax.rem(me[2] + d, n_z)
+
+            @pl.when(negate(both(origin_line, target == 0)))
+            def _():
+                rows_copy(g, d, target, me[2]).start()
 
     def receive(g, d):
         rows_copy(g, d, lax.rem(me[2] + d, n_z), lax.rem(me[2] + n_z - d, n_z)).wait_recv()
@@ -275,7 +333,11 @@
     few = contract(jnp.concatenate(few, axis=0), eye_ref[...]).reshape(n_z, rows, VECS).astype(jnp.bfloat16)
     stage[:, 1] = few
     for g, group in enumerate(GROUPS):
+        if g == 1:
+            to_the_origin(0)
         if g == 2:
+            up()
+            to_the_origin(1)
             for x, y in CROSS:
                 arrive((x, y, 0))
             send(len(GROUPS))
@@ -290,6 +352,15 @@
                 block = jnp.where(inside(o), block, 0.0)
             stage[:, PLACES[ORDER.index(o)]] = block.reshape(n_z, rows, VECS).astype(jnp.bfloat16)
         send(g)
+
+    @pl.when(both(origin_line, negate(origin)))
+    def _():
+        @pl.when(me[2] != 1)
+        def _():
+            pl.semaphore_wait(origin_ready, 1)
+
+        for g in (0, 3, 1, 2):
+            rows_copy(g, n_z - me[2], 0, me[2]).start()
 
     def put(o, source, value):
         out_ref[pl.ds(number(o) * n_z + source, rows, stride=27 * n_z), :] = value
@@ -371,6 +442,8 @@
             pltpu.SemaphoreType.DMA((len(NEIGHBOURS),)),
             pltpu.SemaphoreType.DMA((len(GROUPS) + 1, n_z - 1)),
             pltpu.SemaphoreType.DMA((len(GROUPS) + 1, n_z - 1)),
+            pltpu.SemaphoreType.REGULAR,
+            pltpu.SemaphoreType.REGULAR,
         ],
         compiler_params=pltpu.CompilerParams(collective_id=0, has_side_effects=True, vmem_limit_bytes=24 * 2**20),
         name="coarse",

time: 36.6 us -> 35.2 us (0.962)
  the two profiles are of different devices: /device:TPU:1 before, /device:TPU:2 now
where the time goes in v4:
time: 35.2 us; the launch traced here: 35 us
  Pallas kernels  33.8 us (96%)
  local copies, waits for them, and re-layouts  1.21 us (3%)
    pallas_call x1, Pallas kernels, body(): pl.pallas_call(functools.partial(kernel, sizes), out_shape=jax.ShapeDtype...  33.8 us
    unnamed x1, local copies, waits for them, and re-layouts  1.21 us

profile of v4, /device:TPU:2, one launch (start us, length us, event | category | flops | bytes accessed | tf_op | source)
XLA Modules:
  0.0 35.0 jit_solution(422590240957057082)
XLA Ops:
  0.0 33.8 %coarse.1 = f32[3456,128]{1,0:T(8,128)S(1)} custom-call(bf16[8,48,128]{2,1,0:T(8,128)(2,1)} %bitcast.11, s32[16,8]{1,0:T(8,128)} %bitcast.12, f32[16]{0:T(128)} %mod_in.1, f32[3,3,27]{2,1,0:T(4,128)} %bitcast.13, s32[128,144]{1,0:T(8,128)} %constant.20.clone.index_in, f32[3,27,144]{2,1,0:T(8,128)} %constant.21.clone.widen_in, ...), custom_call_target="tpu_custom_call" | custom-call | tf_op jit(solution)/shard_map/coarse/pallas_call | solution.py:418
  33.8 1.2 %copy.14 = f32[1,1,16,8,27,128]{5,3,4,2,1,0:T(8,128)} copy(f32[1,1,16,8,27,128]{5,3,4,2,1,0:T(8,128)S(1)} %bitcast.10) | data formatting | bytes 3538944

commit v5 on v4

--- a/solution.py
+++ b/solution.py
@@ -95,6 +95,13 @@
     return index, widen, chosen, pack, regroup, place, np.eye(128, dtype=np.float32), choose.reshape(128, 1536)
 
 
+CROSSINGS = (3, 7)
+
+
+def crossing(y):
+    return functools.reduce(jnp.logical_or, [y == k for k in CROSSINGS])
+
+
 def dot(a, b, precision=None):
     return jnp.dot(a, b, preferred_element_type=jnp.float32, precision=precision)
 
@@ -149,15 +156,14 @@
     def except_origin(o):
         return inside(o) if max(o) > 0 else both(inside(o), negate(to_origin(o)))
 
+    below_crossing, above_crossing = crossing(me[1]), crossing(me[1] - 1)
     beside = [o for o in NEIGHBOURS if o[:2] != (0, 0)]
     barrier = pltpu.get_barrier_semaphore()
     expected = jnp.int32(n_z - 1) - both(origin_line, negate(origin)).astype(jnp.int32)
     for o in beside:
-        awaited = both(inside(o), origin) if o[1] > 0 else except_origin(o)
+        awaited = both(inside(o), negate(below_crossing)) if o[1] > 0 else except_origin(o)
         expected = expected + awaited.astype(jnp.int32)
-        told = inside(o) if o[1] >= 0 else to_origin(o)
-        if told is None:
-            continue
+        told = inside(o) if o[1] >= 0 else both(inside(o), negate(above_crossing))
 
         @pl.when(both(told, negate(origin)))
         def _():
@@ -167,6 +173,15 @@
     def _():
         for d in range(1, n_z):
             pl.semaphore_signal(barrier, inc=1, device_id=at((0, 0, d)), device_id_type=MESH)
+
+    @pl.when(origin)
+    def _():
+        pl.semaphore_wait(barrier, expected)
+        for o in beside:
+            if min(o) >= 0:
+                pl.semaphore_signal(origin_ready, inc=1, device_id=at(o), device_id_type=MESH)
+        for d in range(1, n_z):
+            pl.semaphore_signal(origin_ready, inc=1, device_id=at((0, 0, d)), device_id_type=MESH)
 
     for copy in loads[:6]:
         copy.wait()
@@ -190,6 +205,35 @@
     for j in range(4):
         edge[j] = dense[32 * j : 32 * j + 32]
 
+    def halo(r):
+        xi = CX - 1 if r[0] < 0 else 0
+        if r[1] == 0 and r[2] == 0:
+            return xp.at[2 + xi], hx.at[side(r[0])]
+        if r[0] == 0 and r[2] == 0:
+            return pk.at[side(r[1])], hy.at[side(r[1])]
+        if r[0] == 0 and r[1] == 0:
+            return pk.at[2 + side(r[2])], hz.at[side(r[2])]
+        if r[0] == 0:
+            return edge.at[pair(r[1], r[2])], hyz.at[pair(r[1], r[2])]
+        if r[2] == 0:
+            return pk.at[side(r[1]), xi], hxy.at[pair(r[0], r[1])]
+        return pk.at[2 + side(r[2]), xi], hxz.at[pair(r[0], r[2])]
+
+    copies = {}
+    for r in sorted(NEIGHBOURS, key=lambda r: (r[1] == 0, -abs(r[0]) - abs(r[2]))):
+        src, dst = halo(r)
+        k = NEIGHBOURS.index(r)
+        copies[r] = pltpu.make_async_remote_copy(
+            src_ref=src, dst_ref=dst, send_sem=halo_send.at[k], recv_sem=halo_recv.at[k],
+            device_id=at((-r[0], -r[1], -r[2])), device_id_type=MESH,
+        )
+
+    @pl.when(origin)
+    def _():
+        for r in NEIGHBOURS:
+            if max(r) <= 0:
+                copies[r].start()
+
     for copy in loads[6:]:
         copy.wait()
     index = index_ref[...]
@@ -205,47 +249,22 @@
             matrix = jnp.where(index == km * 3 + b, table[16 * b + km : 16 * b + km + 1, :], matrix)
     high = matrix.astype(jnp.bfloat16)
     low = (matrix - high.astype(jnp.float32)).astype(jnp.bfloat16)
-    pl.semaphore_wait(barrier, expected)
+    @pl.when(negate(origin))
+    def _():
+        pl.semaphore_wait(barrier, expected)
+
     for o in beside:
         if o[1] < 0:
 
-            @pl.when(except_origin(o))
+            @pl.when(both(inside(o), above_crossing))
             def _():
                 pl.semaphore_signal(ready, inc=1, device_id=at(o), device_id_type=MESH)
 
-    @pl.when(origin)
-    def _():
-        for o in beside:
-            if min(o) >= 0:
-                pl.semaphore_signal(origin_ready, inc=1, device_id=at(o), device_id_type=MESH)
-        for d in range(1, n_z):
-            pl.semaphore_signal(origin_ready, inc=1, device_id=at((0, 0, d)), device_id_type=MESH)
-
-    def halo(r):
-        xi = CX - 1 if r[0] < 0 else 0
-        if r[1] == 0 and r[2] == 0:
-            return xp.at[2 + xi], hx.at[side(r[0])]
-        if r[0] == 0 and r[2] == 0:
-            return pk.at[side(r[1])], hy.at[side(r[1])]
-        if r[0] == 0 and r[1] == 0:
-            return pk.at[2 + side(r[2])], hz.at[side(r[2])]
-        if r[0] == 0:
-            return edge.at[pair(r[1], r[2])], hyz.at[pair(r[1], r[2])]
-        if r[2] == 0:
-            return pk.at[side(r[1]), xi], hxy.at[pair(r[0], r[1])]
-        return pk.at[2 + side(r[2]), xi], hxz.at[pair(r[0], r[2])]
-
-    copies = {}
-    for r in sorted(NEIGHBOURS, key=lambda r: (r[1] == 0, -abs(r[0]) - abs(r[2]))):
-        src, dst = halo(r)
-        k = NEIGHBOURS.index(r)
-        copies[r] = pltpu.make_async_remote_copy(
-            src_ref=src, dst_ref=dst, send_sem=halo_send.at[k], recv_sem=halo_recv.at[k],
-            device_id=at((-r[0], -r[1], -r[2])), device_id_type=MESH,
-        )
+    for r in NEIGHBOURS:
         o = (-r[0], -r[1], -r[2])
-
-        @pl.when(both(inside(o), origin) if o[1] > 0 else except_origin(o))
+        at_once = both(inside(o), negate(below_crossing)) if o[1] > 0 else except_origin(o)
+
+        @pl.when(both(at_once, negate(origin)))
         def _():
             copies[r].start()
 
@@ -261,13 +280,13 @@
     def up():
         above = [o for o in beside if o[1] > 0]
 
-        @pl.when(both(inside((0, 1, 0)), negate(origin)))
+        @pl.when(below_crossing)
         def _():
             pl.semaphore_wait(ready, sum(inside(o).astype(jnp.int32) for o in above))
 
         for o in above:
 
-            @pl.when(both(inside(o), negate(origin)))
+            @pl.when(both(inside(o), below_crossing))
             def _():
                 copies[-o[0], -o[1], -o[2]].start()
 

time: 35.2 us -> 32.8 us (0.932)
  the two profiles are of different devices: /device:TPU:2 before, /device:TPU:1 now
where the time goes in v5:
time: 32.8 us; the launch traced here: 32.3 us
  Pallas kernels  31.1 us (95%)
  local copies, waits for them, and re-layouts  1.21 us (4%)
    pallas_call x1, Pallas kernels, body(): pl.pallas_call(functools.partial(kernel, sizes), out_shape=jax.ShapeDtype...  31.1 us
    unnamed x1, local copies, waits for them, and re-layouts  1.21 us

profile of v5, /device:TPU:1, one launch (start us, length us, event | category | flops | bytes accessed | tf_op | source)
XLA Modules:
  0.0 32.3 jit_solution(16600518254853065005)
XLA Ops:
  0.0 31.1 %coarse.1 = f32[3456,128]{1,0:T(8,128)S(1)} custom-call(bf16[8,48,128]{2,1,0:T(8,128)(2,1)} %bitcast.11, s32[16,8]{1,0:T(8,128)} %bitcast.12, f32[16]{0:T(128)} %mod_in.1, f32[3,3,27]{2,1,0:T(4,128)} %bitcast.13, s32[128,144]{1,0:T(8,128)} %constant.20.clone.index_in, f32[3,27,144]{2,1,0:T(8,128)} %constant.21.clone.widen_in, ...), custom_call_target="tpu_custom_call" | custom-call | tf_op jit(solution)/shard_map/coarse/pallas_call | solution.py:437
  31.1 1.2 %copy.14 = f32[1,1,16,8,27,128]{5,3,4,2,1,0:T(8,128)} copy(f32[1,1,16,8,27,128]{5,3,4,2,1,0:T(8,128)S(1)} %bitcast.10) | data formatting | bytes 3538944

commit v6 on v5

--- a/solution.py
+++ b/solution.py
@@ -75,11 +75,13 @@
         if row is not None:
             y, z, a = row
             pack[r, (y % CY) * 12 + a * 4 + z % CZ] = 1
-    regroup = np.zeros((128, 128), np.float32)
-    for j in range(4):
-        for x in range(CX):
-            for b in range(4):
-                regroup[j * 32 + x * 4 + b, x * 16 + j * 4 + b] = 1
+    regroup = np.zeros((2, 96, 128), np.float32)
+    for x in range(CX):
+        for j in range(4):
+            for b in range(3):
+                regroup[0, j * 24 + x * 3 + b, x * 16 + j * 4 + b] = 1
+        for j in range(12):
+            regroup[1, x * 12 + j, x * 16 + j] = 1
     place = np.zeros((PLANE, 16), np.float32)
     for y in range(CY):
         for a in range(3):
@@ -115,7 +117,7 @@
     vec_in, mat_in, mod_in, sten_in, index_in, widen_in, chosen_in, pack_in, regroup_in, place_in, eye_in, choose_in,
     out_ref,
     vec_ref, mat_ref, mod_ref, sten_ref, index_ref, widen_ref, chosen_ref, pack_ref, regroup_ref, place_ref, eye_ref, choose_ref, load_sem,
-    xp, pk, edge, hx, hy, hz, hyz, hxy, hxz, ic, iyz, icn, ie, stage, recv, cells,
+    xp, pk, edge, face, iface, hx, hy, hz, hyz, hxy, hxz, ic, iyz, icn, ie, stage, recv, cells,
     halo_send, halo_recv, row_send, row_recv, ready, origin_ready,
 ):
     loads = [
@@ -201,18 +203,19 @@
         packed = dot(pack_ref[...], plane)
         for k in range(5):
             pk[k, x] = packed[16 * k : 16 * k + 16].astype(jnp.bfloat16)
-    dense = dot(regroup_ref[...], pk[4].reshape(CX * 16, VECS)).astype(jnp.bfloat16)
+    dense = dot(regroup_ref[0], pk[4].reshape(CX * 16, VECS))
     for j in range(4):
-        edge[j] = dense[32 * j : 32 * j + 32]
+        edge[j] = dense[24 * j : 24 * j + 24].astype(jnp.bfloat16)
+        face[j] = dot(regroup_ref[1], pk[j].reshape(CX * 16, VECS)).astype(jnp.bfloat16)
 
     def halo(r):
         xi = CX - 1 if r[0] < 0 else 0
         if r[1] == 0 and r[2] == 0:
             return xp.at[2 + xi], hx.at[side(r[0])]
         if r[0] == 0 and r[2] == 0:
-            return pk.at[side(r[1])], hy.at[side(r[1])]
+            return face.at[side(r[1])], hy.at[side(r[1])]
         if r[0] == 0 and r[1] == 0:
-            return pk.at[2 + side(r[2])], hz.at[side(r[2])]
+            return face.at[2 + side(r[2])], hz.at[side(r[2])]
         if r[0] == 0:
             return edge.at[pair(r[1], r[2])], hyz.at[pair(r[1], r[2])]
         if r[2] == 0:
@@ -233,6 +236,47 @@
         for r in NEIGHBOURS:
             if max(r) <= 0:
                 copies[r].start()
+
+    @pl.when(negate(origin))
+    def _():
+        pl.semaphore_wait(barrier, expected)
+
+    for o in beside:
+        if o[1] < 0:
+
+            @pl.when(both(inside(o), above_crossing))
+            def _():
+                pl.semaphore_signal(ready, inc=1, device_id=at(o), device_id_type=MESH)
+
+    for r in NEIGHBOURS:
+        o = (-r[0], -r[1], -r[2])
+        at_once = both(inside(o), negate(below_crossing)) if o[1] > 0 else except_origin(o)
+
+        @pl.when(both(at_once, negate(origin)))
+        def _():
+            copies[r].start()
+
+    def to_the_origin(level):
+        for r in NEIGHBOURS:
+            if min(r) >= 0 and r[1] == level:
+
+                @pl.when(to_origin((-r[0], -r[1], -r[2])))
+                def _():
+                    pl.semaphore_wait(origin_ready, 1)
+                    copies[r].start()
+
+    def up():
+        above = [o for o in beside if o[1] > 0]
+
+        @pl.when(below_crossing)
+        def _():
+            pl.semaphore_wait(ready, sum(inside(o).astype(jnp.int32) for o in above))
+
+        for o in above:
+
+            @pl.when(both(inside(o), below_crossing))
+            def _():
+                copies[-o[0], -o[1], -o[2]].start()
 
     for copy in loads[6:]:
         copy.wait()
@@ -249,47 +293,6 @@
             matrix = jnp.where(index == km * 3 + b, table[16 * b + km : 16 * b + km + 1, :], matrix)
     high = matrix.astype(jnp.bfloat16)
     low = (matrix - high.astype(jnp.float32)).astype(jnp.bfloat16)
-    @pl.when(negate(origin))
-    def _():
-        pl.semaphore_wait(barrier, expected)
-
-    for o in beside:
-        if o[1] < 0:
-
-            @pl.when(both(inside(o), above_crossing))
-            def _():
-                pl.semaphore_signal(ready, inc=1, device_id=at(o), device_id_type=MESH)
-
-    for r in NEIGHBOURS:
-        o = (-r[0], -r[1], -r[2])
-        at_once = both(inside(o), negate(below_crossing)) if o[1] > 0 else except_origin(o)
-
-        @pl.when(both(at_once, negate(origin)))
-        def _():
-            copies[r].start()
-
-    def to_the_origin(level):
-        for r in NEIGHBOURS:
-            if min(r) >= 0 and r[1] == level:
-
-                @pl.when(to_origin((-r[0], -r[1], -r[2])))
-                def _():
-                    pl.semaphore_wait(origin_ready, 1)
-                    copies[r].start()
-
-    def up():
-        above = [o for o in beside if o[1] > 0]
-
-        @pl.when(below_crossing)
-        def _():
-            pl.semaphore_wait(ready, sum(inside(o).astype(jnp.int32) for o in above))
-
-        for o in above:
-
-            @pl.when(both(inside(o), below_crossing))
-            def _():
-                copies[-o[0], -o[1], -o[2]].start()
-
     for i in range(CX + 2):
         window = xp[i : i + 3].reshape(3 * PLANE, VECS)
         image = (dot(high, window) + dot(low, window)).astype(jnp.bfloat16)
@@ -297,9 +300,10 @@
         for k in range(4):
             iyz[k, i] = image[48 + 16 * k : 64 + 16 * k]
         icn[i] = image[112:128]
-    dense = dot(regroup_ref[...], icn[1 : CX + 1].reshape(CX * 16, VECS)).astype(jnp.bfloat16)
+    dense = dot(regroup_ref[0], icn[1 : CX + 1].reshape(CX * 16, VECS))
     for j in range(4):
-        ie[j] = dense[32 * j : 32 * j + 32]
+        ie[j] = dense[24 * j : 24 * j + 24].astype(jnp.bfloat16)
+        iface[j] = dot(regroup_ref[1], iyz[j, 1 : CX + 1].reshape(CX * 16, VECS)).astype(jnp.bfloat16)
 
     def operands(o):
         xi = 0 if o[0] < 0 else CX + 1
@@ -309,11 +313,9 @@
         if o[1] == 0 and o[2] == 0:
             return ic[xi], hx[side(o[0])]
         if o[0] == 0 and o[2] == 0:
-            k = side(o[1])
-            return iyz[k, inner].reshape(CX * 16, VECS), hy[k].reshape(CX * 16, VECS)
+            return iface[side(o[1])], hy[side(o[1])]
         if o[0] == 0 and o[1] == 0:
-            k = side(o[2])
-            return iyz[2 + k, inner].reshape(CX * 16, VECS), hz[k].reshape(CX * 16, VECS)
+            return iface[2 + side(o[2])], hz[side(o[2])]
         if o[0] == 0:
             k = pair(o[1], o[2])
             return ie[k], hyz[k]
@@ -443,17 +445,19 @@
             pltpu.SemaphoreType.DMA((len(operands),)),
             pltpu.VMEM((CX + 4, PLANE, VECS), b16),
             pltpu.VMEM((5, CX, 16, VECS), b16),
-            pltpu.VMEM((4, 32, VECS), b16),
+            pltpu.VMEM((4, 24, VECS), b16),
+            pltpu.VMEM((4, 96, VECS), b16),
+            pltpu.VMEM((4, 96, VECS), b16),
             pltpu.VMEM((2, PLANE, VECS), b16),
-            pltpu.VMEM((2, CX, 16, VECS), b16),
-            pltpu.VMEM((2, CX, 16, VECS), b16),
-            pltpu.VMEM((4, 32, VECS), b16),
+            pltpu.VMEM((2, 96, VECS), b16),
+            pltpu.VMEM((2, 96, VECS), b16),
+            pltpu.VMEM((4, 24, VECS), b16),
             pltpu.VMEM((4, 16, VECS), b16),
             pltpu.VMEM((4, 16, VECS), b16),
             pltpu.VMEM((CX + 2, PLANE, VECS), b16),
             pltpu.VMEM((4, CX + 2, 16, VECS), b16),
             pltpu.VMEM((CX + 2, 16, VECS), b16),
-            pltpu.VMEM((4, 32, VECS), b16),
+            pltpu.VMEM((4, 24, VECS), b16),
             pltpu.VMEM((n_z, 16, rows, VECS), b16),
             pltpu.VMEM((n_z, 16, rows, VECS), b16),
             pltpu.VMEM((n_z, 4, 16, VECS), b16),

time: 32.8 us -> 31.8 us (0.970)
  Pallas kernels: 31.1 us -> 30.4 us
    pallas_call x1, Pallas kernels: 31.1 us -> 30.4 us  [body(): pl.pallas_call(functools.partial(kernel, sizes), out_shape=jax.ShapeDtype...]
where the time goes in v6:
time: 31.8 us; the launch traced here: 31.6 us
  Pallas kernels  30.4 us (96%)
  local copies, waits for them, and re-layouts  1.21 us (4%)
    pallas_call x1, Pallas kernels, body(): pl.pallas_call(functools.partial(kernel, sizes), out_shape=jax.ShapeDtype...  30.4 us
    unnamed x1, local copies, waits for them, and re-layouts  1.21 us

profile of v6, /device:TPU:1, one launch (start us, length us, event | category | flops | bytes accessed | tf_op | source)
XLA Modules:
  0.0 31.6 jit_solution(13717118687209502988)
XLA Ops:
  0.0 30.4 %coarse.1 = f32[3456,128]{1,0:T(8,128)S(1)} custom-call(bf16[8,48,128]{2,1,0:T(8,128)(2,1)} %bitcast.11, s32[16,8]{1,0:T(8,128)} %bitcast.12, f32[16]{0:T(128)} %mod_in.1, f32[3,3,27]{2,1,0:T(4,128)} %bitcast.13, s32[128,144]{1,0:T(8,128)} %constant.20.clone.index_in, f32[3,27,144]{2,1,0:T(8,128)} %constant.21.clone.widen_in, ...), custom_call_target="tpu_custom_call" | custom-call | tf_op jit(solution)/shard_map/coarse/pallas_call | solution.py:439
  30.4 1.2 %copy.14 = f32[1,1,16,8,27,128]{5,3,4,2,1,0:T(8,128)} copy(f32[1,1,16,8,27,128]{5,3,4,2,1,0:T(8,128)S(1)} %bitcast.10) | data formatting | bytes 3538944

commit v7 on v6

--- a/solution.py
+++ b/solution.py
@@ -300,11 +300,6 @@
         for k in range(4):
             iyz[k, i] = image[48 + 16 * k : 64 + 16 * k]
         icn[i] = image[112:128]
-    dense = dot(regroup_ref[0], icn[1 : CX + 1].reshape(CX * 16, VECS))
-    for j in range(4):
-        ie[j] = dense[24 * j : 24 * j + 24].astype(jnp.bfloat16)
-        iface[j] = dot(regroup_ref[1], iyz[j, 1 : CX + 1].reshape(CX * 16, VECS)).astype(jnp.bfloat16)
-
     def operands(o):
         xi = 0 if o[0] < 0 else CX + 1
         inner = slice(1, CX + 1)
@@ -355,6 +350,10 @@
     stage[:, 1] = few
     for g, group in enumerate(GROUPS):
         if g == 1:
+            dense = dot(regroup_ref[0], icn[1 : CX + 1].reshape(CX * 16, VECS))
+            for j in range(4):
+                ie[j] = dense[24 * j : 24 * j + 24].astype(jnp.bfloat16)
+                iface[j] = dot(regroup_ref[1], iyz[j, 1 : CX + 1].reshape(CX * 16, VECS)).astype(jnp.bfloat16)
             to_the_origin(0)
         if g == 2:
             up()

time: 31.8 us -> 31.8 us (level)
  no operation moved by 1% of the time
where the time goes in v7:
time: 31.8 us; the launch traced here: 31.6 us
  Pallas kernels  30.4 us (96%)
  local copies, waits for them, and re-layouts  1.21 us (4%)
    pallas_call x1, Pallas kernels, body(): pl.pallas_call(functools.partial(kernel, sizes), out_shape=jax.ShapeDtype...  30.4 us
    unnamed x1, local copies, waits for them, and re-layouts  1.21 us

profile of v7, /device:TPU:1, one launch (start us, length us, event | category | flops | bytes accessed | tf_op | source)
XLA Modules:
  0.0 31.6 jit_solution(4585858383557958154)
XLA Ops:
  0.0 30.4 %coarse.1 = f32[3456,128]{1,0:T(8,128)S(1)} custom-call(bf16[8,48,128]{2,1,0:T(8,128)(2,1)} %bitcast.11, s32[16,8]{1,0:T(8,128)} %bitcast.12, f32[16]{0:T(128)} %mod_in.1, f32[3,3,27]{2,1,0:T(4,128)} %bitcast.13, s32[128,144]{1,0:T(8,128)} %constant.20.clone.index_in, f32[3,27,144]{2,1,0:T(8,128)} %constant.21.clone.widen_in, ...), custom_call_target="tpu_custom_call" | custom-call | tf_op jit(solution)/shard_map/coarse/pallas_call | solution.py:438
  30.4 1.2 %copy.14 = f32[1,1,16,8,27,128]{5,3,4,2,1,0:T(8,128)} copy(f32[1,1,16,8,27,128]{5,3,4,2,1,0:T(8,128)S(1)} %bitcast.10) | data formatting | bytes 3538944
